TPU v7x, 32 devices: a whole 2x2x4 slice. The times are simulated.
32 devices in a mesh: row: 8 (over z, y), col: 4 (over x, core).
Axes of the slice: x: 2, y: 2, z: 4, core: 2. Of those that a mesh axis runs over, the one named last changes fastest.
Arguments:
- leaf_inverse: bfloat16 [32, 1024, 1024], P(('row', 'col')), as said below
- leaf_rhs: bfloat16 [32, 1024, 512], P(('row', 'col')), may hold values from -6 to 6
- leaf_tiles: bfloat16 [32, 1024, 1024], P(('row', 'col')), may hold values from -0.09375 to 0.09375
- mid_inverse_t: bfloat16 [8, 1024, 1024], P('col', None, 'row'), as said below
- mid_rhs: bfloat16 [8, 1024, 512], P('col', 'row'), may hold values from -6 to 6
- mid_tiles: bfloat16 [8, 1024, 1024], P('col', None, 'row'), may hold values from -0.125 to 0.125
- top_inverse_t: bfloat16 [2, 1024, 1024], P(None, None, 'col'), as said below
- top_rhs: bfloat16 [2, 1024, 512], P(None, 'col'), may hold values from -6 to 6
- tile_lists: int32 [32, 1], P(('row', 'col')), may hold values from 0 to 1
Outputs:
- leaf_solved: bfloat16 [32, 1024, 512], P(('row', 'col'))
- mid_solved: bfloat16 [8, 1024, 512], P('col', 'row')
- top_solved: bfloat16 [2, 1024, 512], P(None, 'col')
Inputs may be any that keep to these rules, and one draw needn't show every extreme that they name: Each leaf_inverse[d] is zero above its diagonal and has diagonal entries between 0.75 and 1.25. Each mid_inverse_t[q] is zero below its diagonal and has diagonal entries between 0.75 and 1.25. Each top_inverse_t[b] is zero below its diagonal and has diagonal entries between 0.75 and 1.25.
All inputs are finite; a program needn't handle non-finite values.
Results may differ from a plain program's by a relative error of at most 0.0065.
Values may be sent and summed in bfloat16 or wider, within the bound.
No kernel may reach another device: no remote copies, remote signals or barrier semaphores. Data moves between devices by JAX's collectives and lax.ppermute only.
A program may use at most 64 MiB of HBM per device.

v0:
```python
import jax
import jax.numpy as jnp
from jax import lax
from jax.sharding import PartitionSpec as P

NB = 2


def solve_piece(inverse_cols, piece):
    return lax.dot_general(
        inverse_cols, piece, (((1,), (1,)), ((0,), (0,))), preferred_element_type=jnp.float32
    )


def local(
    leaf_inverse,
    leaf_rhs,
    leaf_tiles,
    mid_inverse_t,
    mid_rhs,
    mid_tiles,
    top_inverse_t,
    top_rhs,
    tile_lists,
):
    slot_ids = jnp.arange(NB, dtype=jnp.int32)[:, None, None]
    solved_leaf = jnp.dot(leaf_inverse[0], leaf_rhs[0], preferred_element_type=jnp.float32).astype(
        jnp.bfloat16
    )
    leaf_update = jnp.dot(leaf_tiles[0], solved_leaf, preferred_element_type=jnp.float32)
    mid_terms = jnp.where(slot_ids == tile_lists[0, 0], leaf_update[None], 0.0)
    mid_share = lax.psum_scatter(mid_terms, "row", scatter_dimension=1, tiled=True)
    mid_resid = (mid_rhs.astype(jnp.float32) - mid_share).astype(jnp.bfloat16)
    mid_own = solve_piece(
        mid_inverse_t, lax.all_gather(mid_resid, "row", axis=1, tiled=True)
    ).astype(jnp.bfloat16)
    top_terms = lax.dot_general(
        mid_tiles, mid_own, (((2,), (1,)), ((0,), (0,))), preferred_element_type=jnp.float32
    )
    summed_rows = lax.psum(top_terms, "row")
    top_share = lax.psum_scatter(summed_rows, "col", scatter_dimension=1, tiled=True)
    top_resid = (top_rhs.astype(jnp.float32) - top_share).astype(jnp.bfloat16)
    top_own = solve_piece(
        top_inverse_t, lax.all_gather(top_resid, "col", axis=1, tiled=True)
    ).astype(jnp.bfloat16)
    return (solved_leaf[None], mid_own, top_own)


def solution(mesh):
    placed = (
        P(("row", "col"), None, None),
        P(("row", "col"), None, None),
        P(("row", "col"), None, None),
        P("col", None, "row"),
        P("col", "row", None),
        P("col", None, "row"),
        P(None, None, "col"),
        P(None, "col", None),
        P(("row", "col"), None),
    )
    return jax.shard_map(
        local,
        mesh=mesh,
        in_specs=placed,
        out_specs=(P(("row", "col"), None, None), P("col", "row", None), P(None, "col", None)),
        check_vma=False,
    )
```

profile of v0, /device:TPU:0, one launch (start us, length us, event | category | flops | bytes accessed | tf_op | source)
XLA Modules:
  0.0 324.7 jit_solution(155862839401762226)
XLA Ops:
  7.2 0.0 copy-start
  7.2 0.0 reduce-scatter.3.cloned.1.call-start
  8.0 0.8 copy-done
  8.8 2.6 fusion.7
  11.4 0.0 copy-start.5
  11.4 1.0 copy-done.5
  12.4 1.3 fusion.4
  13.7 2.5 broadcast_select_fusion
  16.2 0.0 reduce-scatter.3.cloned.1.call-update
  16.2 0.0 all-gather.3.cloned.1.call-start
  16.3 0.9 copy-done.3
  17.2 0.2 copy.12
  17.4 90.4 %reduce-scatter.3.cloned.1.call-done = f32[2,128,512]{1,2,0:T(8,128)} async-done(((f32[2,1024,512]{1,2,0:T(8,128)}), f32[2,128,512]{1,2,0:T(8,128)}) %reduce-scatter.3.cloned.1.call-update) | async-done | bytes 524304 | tf_op jit(solution)/shard_map/reduce_scatter | solution.py:32
  107.8 1.8 subtract_convert_fusion.1
  109.6 0.0 all-gather.3.cloned.1.call-update
  109.6 0.0 reduce-scatter.5.cloned.1.call-start
  109.7 50.8 %all-gather.3.cloned.1.call-done = bf16[2,1024,512]{1,2,0:T(8,128)(2,1)} async-done(((bf16[2,128,512]{1,2,0:T(8,128)(2,1)}), bf16[2,1024,512]{1,2,0:T(8,128)(2,1)}) %all-gather.3.cloned.1.call-update) | async-done | bytes 2097168 | tf_op jit(solution)/shard_map/all_gather | solution.py:35
  160.4 2.4 convolution_convert_fusion.1
  162.8 2.7 convolution_bitcast_fusion
  165.5 0.0 reduce-scatter.5.cloned.1.call-update
  165.5 0.0 all-reduce.2.cloned.1.call-start
  165.5 42.7 %reduce-scatter.5.cloned.1.call-done = f32[2,256,512]{1,2,0:T(8,128)} async-done(((f32[2,1024,512]{1,2,0:T(8,128)}), f32[2,256,512]{1,2,0:T(8,128)}) %reduce-scatter.5.cloned.1.call-update) | async-done | bytes 1048592 | tf_op jit(solution)/shard_map/reduce_scatter | solution.py:41
  208.2 0.0 all-reduce.2.cloned.1.call-update
  208.3 0.0 all-gather.5.cloned.1.call-start
  208.3 0.2 copy.13
  208.5 81.3 %all-reduce.2.cloned.1.call-done = f32[2,256,512]{1,2,0:T(8,128)} async-done(((f32[2,256,512]{1,2,0:T(8,128)}), f32[2,256,512]{1,2,0:T(8,128)}) %all-reduce.2.cloned.1.call-update) | async-done | bytes 1048592 | tf_op jit(solution)/shard_map/psum | solution.py:40
  289.8 2.1 subtract_convert_fusion
  292.0 0.0 all-gather.5.cloned.1.call-update
  292.0 0.9 copy.14
  292.8 21.7 %all-gather.5.cloned.1.call-done = bf16[2,1024,512]{1,2,0:T(8,128)(2,1)} async-done(((bf16[2,256,512]{1,2,0:T(8,128)(2,1)}), bf16[2,1024,512]{1,2,0:T(8,128)(2,1)}) %all-gather.5.cloned.1.call-update) | async-done | bytes 2097168 | tf_op jit(solution)/shard_map/all_gather | solution.py:44
  314.6 2.6 fusion.10
  317.1 1.0 copy.15
  (8 shorter events, 0.0 us)
Async XLA Ops:
  7.2 1.6 copy-start
  7.2 100.6 %reduce-scatter.3.cloned.1.call-start = ((), (), s32[]{:S(2)}) async-start(), calls=%async_computation.2 | async-start | bytes 4718592 | tf_op jit(solution)/shard_map/reduce_scatter | solution.py:32
  8.8 3.6 %copy-start.4 = (bf16[1,1024,1024]{2,1,0:T(8,128)(2,1)S(1)}, bf16[1,1024,1024]{2,1,0:T(8,128)(2,1)}, u32[]{:S(2)}) copy-start(bf16[1,1024,1024]{2,1,0:T(8,128)(2,1)} %param.11) | copy-start | bytes 6291460
  11.4 1.0 copy-start.5
  16.2 0.9 copy-start.3
  16.2 144.2 %all-gather.3.cloned.1.call-start = ((), (), s32[]{:S(2)}) async-start(), calls=%async_computation.3 | async-start | bytes 2359296 | tf_op jit(solution)/shard_map/all_gather | solution.py:35
  17.3 145.5 %copy-start.1 = (bf16[2,1024,128]{2,1,0:T(8,128)(2,1)S(1)}, bf16[2,1024,128]{2,1,0:T(8,128)(2,1)}, u32[]{:S(2)}) copy-start(bf16[2,1024,128]{2,1,0:T(8,128)(2,1)} %param.14) | copy-start | bytes 1572868
  109.6 98.6 %reduce-scatter.5.cloned.1.call-start = ((), (), s32[]{:S(2)}) async-start(), calls=%async_computation.5 | async-start | bytes 5242880 | tf_op jit(solution)/shard_map/reduce_scatter | solution.py:41
  165.5 42.8 %copy-start.2 = (bf16[2,256,512]{2,1,0:T(8,128)(2,1)S(1)}, bf16[2,256,512]{2,1,0:T(8,128)(2,1)}, u32[]{:S(2)}) copy-start(bf16[2,256,512]{2,1,0:T(8,128)(2,1)} %param.16) | copy-start | bytes 1572868
  165.5 124.3 %all-reduce.2.cloned.1.call-start = ((), (), s32[]{:S(2)}) async-start(), calls=%async_computation.6 | async-start | bytes 2097152 | tf_op jit(solution)/shard_map/psum | solution.py:40
  208.3 106.3 %all-gather.5.cloned.1.call-start = ((), (), s32[]{:S(2)}) async-start(), calls=%async_computation.4 | async-start | bytes 2621440 | tf_op jit(solution)/shard_map/all_gather | solution.py:44
Sparse Core Ops, SparseCore 0:
  16.4 91.3 reduce-scatter.2
  110.4 49.9 all-gather.2
  165.6 42.5 reduce-scatter.4
  211.6 78.1 all-reduce.1
  292.1 22.3 all-gather.4
where the time goes:
time: 325 us
  waiting for transfers between devices  287 us (88%)
  between operations  14.6 us (4%)
  matrix products  11.5 us (4%)
  other arithmetic  6.48 us (2%)
  local copies, waits for them, and re-layouts  4.84 us (1%)
    reduce_scatter x1, waiting for transfers between devices, local(): lax.psum_scatter(mid_terms, 'row', scatter_dimension=1, tiled=True)  90.4 us
    psum x1, waiting for transfers between devices, local(): summed_rows = lax.psum(top_terms, 'row')  81.3 us
    all_gather x1, waiting for transfers between devices, local(): lax.all_gather(mid_resid, 'row', axis=1, tiled=True)  50.8 us
    reduce_scatter x1, waiting for transfers between devices, local(): lax.psum_scatter(summed_rows, 'col', scatter_dimension=1, tiled=True)  42.7 us
    all_gather x1, waiting for transfers between devices, local(): lax.all_gather(top_resid, 'col', axis=1, tiled=True)  21.7 us
  transfers between devices with their start and end apart: 5, of which 5 were waited for; matrix products, arithmetic and copies ran while one was open for 0% of the time, Pallas kernels for 0%

commit v1 on v0

--- a/solution.py
+++ b/solution.py
@@ -41,7 +41,7 @@
     top_share = lax.psum_scatter(summed_rows, "col", scatter_dimension=1, tiled=True)
     top_resid = (top_rhs.astype(jnp.float32) - top_share).astype(jnp.bfloat16)
     top_own = solve_piece(
-        top_inverse_t, lax.all_gather(top_resid, "col", axis=1, tiled=True)
+        top_inverse_t, jnp.concatenate(lax.all_gather(top_resid, "col"), axis=1)
     ).astype(jnp.bfloat16)
     return (solved_leaf[None], mid_own, top_own)
 

time: 325 us -> 334 us (1.028)
  local copies, waits for them, and re-layouts: 4.84 us -> 14.6 us
    reshape x0 -> x1, local copies, waits for them, and re-layouts: none -> 4.43 us  [local(): jnp.concatenate(lax.all_gather(top_resid, 'col'), axis=1)]
    all_gather x0 -> x1, local copies, waits for them, and re-layouts: none -> 4.28 us  [local(): lax.all_gather(top_resid, 'col')]
where the time goes in v1:
time: 334 us; the launch traced here: 333 us
  waiting for transfers between devices  287 us (86%)
  local copies, waits for them, and re-layouts  14.6 us (4%)
  between operations  14.6 us (4%)
  matrix products  11.4 us (3%)
  other arithmetic  5.68 us (2%)
    reduce_scatter x1, waiting for transfers between devices, local(): lax.psum_scatter(mid_terms, 'row', scatter_dimension=1, tiled=True)  90.4 us
    psum x1, waiting for transfers between devices, local(): summed_rows = lax.psum(top_terms, 'row')  81.4 us
    all_gather x1, waiting for transfers between devices, local(): lax.all_gather(mid_resid, 'row', axis=1, tiled=True)  50.8 us
    reduce_scatter x1, waiting for transfers between devices, local(): lax.psum_scatter(summed_rows, 'col', scatter_dimension=1, tiled=True)  42.7 us
    all_gather x1, waiting for transfers between devices, local(): lax.all_gather(top_resid, 'col')  21.5 us
  transfers between devices with their start and end apart: 5, of which 5 were waited for; matrix products, arithmetic and copies ran while one was open for 0% of the time, Pallas kernels for 0%

profile of v1, /device:TPU:0, one launch (start us, length us, event | category | flops | bytes accessed | tf_op | source)
XLA Modules:
  0.0 333.3 jit_solution(2649638979142680234)
XLA Ops:
  7.2 0.0 reduce-scatter.3.cloned.1.call-start
  8.0 0.8 copy-done
  8.8 2.6 fusion.7
  11.4 1.0 copy-done.6
  12.4 1.3 fusion.4
  13.7 2.5 broadcast_select_fusion
  16.2 0.0 reduce-scatter.3.cloned.1.call-update
  16.2 0.0 all-gather.4.cloned.1.call-start
  16.3 0.9 copy-done.3
  17.2 0.2 copy.17
  17.4 90.4 %reduce-scatter.3.cloned.1.call-done = f32[2,128,512]{1,2,0:T(8,128)} async-done(((f32[2,1024,512]{1,2,0:T(8,128)}), f32[2,128,512]{1,2,0:T(8,128)}) %reduce-scatter.3.cloned.1.call-update) | async-done | bytes 524304 | tf_op jit(solution)/shard_map/reduce_scatter | solution.py:32
  107.8 1.8 subtract_convert_fusion.1
  109.6 0.0 all-gather.4.cloned.1.call-update
  109.6 0.0 reduce-scatter.5.cloned.1.call-start
  109.7 50.8 %all-gather.4.cloned.1.call-done = bf16[2,1024,512]{1,2,0:T(8,128)(2,1)} async-done(((bf16[2,128,512]{1,2,0:T(8,128)(2,1)}), bf16[2,1024,512]{1,2,0:T(8,128)(2,1)}) %all-gather.4.cloned.1.call-update) | async-done | bytes 2097168 | tf_op jit(solution)/shard_map/all_gather | solution.py:35
  160.4 2.3 convolution_convert_fusion.1
  162.7 2.7 convolution_bitcast_fusion
  165.4 0.0 reduce-scatter.5.cloned.1.call-update
  165.4 0.0 all-reduce.2.cloned.1.call-start
  165.5 42.7 %reduce-scatter.5.cloned.1.call-done = f32[2,256,512]{1,2,0:T(8,128)} async-done(((f32[2,1024,512]{1,2,0:T(8,128)}), f32[2,256,512]{1,2,0:T(8,128)}) %reduce-scatter.5.cloned.1.call-update) | async-done | bytes 1048592 | tf_op jit(solution)/shard_map/reduce_scatter | solution.py:41
  208.2 0.0 all-reduce.2.cloned.1.call-update
  208.2 0.0 all-gather.6.cloned.1.call-start
  208.2 0.2 copy.18
  208.4 81.4 %all-reduce.2.cloned.1.call-done = f32[2,256,512]{1,2,0:T(8,128)} async-done(((f32[2,256,512]{1,2,0:T(8,128)}), f32[2,256,512]{1,2,0:T(8,128)}) %all-reduce.2.cloned.1.call-update) | async-done | bytes 1048592 | tf_op jit(solution)/shard_map/psum | solution.py:40
  289.8 1.3 subtract_convert_fusion
  291.2 1.0 copy.19
  292.2 0.9 copy.21
  293.0 21.5 %all-gather.6.cloned.1.call-done = bf16[8,256,512]{2,1,0:T(8,128)(2,1)} async-done(((bf16[2,256,512]{2,1,0:T(8,128)(2,1)}), bf16[8,256,512]{2,1,0:T(8,128)(2,1)}) %all-gather.6.cloned.1.call-update) | async-done | bytes 2097168 | tf_op jit(solution)/shard_map/all_gather | solution.py:44
  314.5 4.3 %copy.20 = bf16[4,2,256,512]{2,0,3,1:T(4,128)(2,1)} copy(bf16[4,2,256,512]{3,2,1,0:T(8,128)(2,1)} %bitcast.35) | data formatting | bytes 4194304 | tf_op jit(solution)/shard_map/all_gather | solution.py:44
  318.8 4.4 %reshape.19 = bf16[2,1024,512]{1,2,0:T(8,128)(2,1)} reshape(bf16[2,4,256,512]{2,1,3,0:T(4,128)(2,1)} %bitcast.34) | data formatting | bytes 4194304 | tf_op jit(solution)/shard_map/reshape | solution.py:44
  323.2 2.6 fusion.10
  325.8 1.0 copy.22
  (13 shorter events, 0.1 us)
Async XLA Ops:
  7.2 1.6 copy-start
  7.2 100.6 %reduce-scatter.3.cloned.1.call-start = ((), (), s32[]{:S(2)}) async-start(), calls=%async_computation.2 | async-start | bytes 4718592 | tf_op jit(solution)/shard_map/reduce_scatter | solution.py:32
  8.8 3.6 %copy-start.4 = (bf16[1,1024,1024]{2,1,0:T(8,128)(2,1)S(1)}, bf16[1,1024,1024]{2,1,0:T(8,128)(2,1)}, u32[]{:S(2)}) copy-start(bf16[1,1024,1024]{2,1,0:T(8,128)(2,1)} %param.11) | copy-start | bytes 6291460
  11.4 1.0 copy-start.6
  16.2 0.9 copy-start.3
  16.2 144.2 %copy-start.5 = (bf16[2,1024,128]{2,1,0:T(8,128)(2,1)S(1)}, bf16[2,1024,128]{2,1,0:T(8,128)(2,1)}, u32[]{:S(2)}) copy-start(bf16[2,1024,128]{2,1,0:T(8,128)(2,1)} %param.12) | copy-start | bytes 1572868
  16.2 144.2 %all-gather.4.cloned.1.call-start = ((), (), s32[]{:S(2)}) async-start(), calls=%async_computation.3 | async-start | bytes 2359296 | tf_op jit(solution)/shard_map/all_gather | solution.py:35
  17.3 145.4 %copy-start.1 = (bf16[2,1024,128]{2,1,0:T(8,128)(2,1)S(1)}, bf16[2,1024,128]{2,1,0:T(8,128)(2,1)}, u32[]{:S(2)}) copy-start(bf16[2,1024,128]{2,1,0:T(8,128)(2,1)} %param.14) | copy-start | bytes 1572868
  109.6 98.5 %reduce-scatter.5.cloned.1.call-start = ((), (), s32[]{:S(2)}) async-start(), calls=%async_computation.5 | async-start | bytes 5242880 | tf_op jit(solution)/shard_map/reduce_scatter | solution.py:41
  165.4 42.8 %copy-start.2 = (bf16[2,256,512]{2,1,0:T(8,128)(2,1)S(1)}, bf16[2,256,512]{2,1,0:T(8,128)(2,1)}, u32[]{:S(2)}) copy-start(bf16[2,256,512]{2,1,0:T(8,128)(2,1)} %param.16) | copy-start | bytes 1572868
  165.4 124.4 %all-reduce.2.cloned.1.call-start = ((), (), s32[]{:S(2)}) async-start(), calls=%async_computation.6 | async-start | bytes 2097152 | tf_op jit(solution)/shard_map/psum | solution.py:40
  208.2 106.3 %all-gather.6.cloned.1.call-start = ((), (), s32[]{:S(2)}) async-start(), calls=%async_computation.4 | async-start | bytes 2621440 | tf_op jit(solution)/shard_map/all_gather | solution.py:44
Sparse Core Ops, SparseCore 0:
  16.4 91.3 reduce-scatter.2
  110.4 49.9 all-gather.3
  165.5 42.5 reduce-scatter.4
  211.5 78.2 all-reduce.1
  292.3 22.1 all-gather.5

commit v2 on v0

--- a/solution.py
+++ b/solution.py
@@ -37,7 +37,11 @@
     top_terms = lax.dot_general(
         mid_tiles, mid_own, (((2,), (1,)), ((0,), (0,))), preferred_element_type=jnp.float32
     )
-    summed_rows = lax.psum(top_terms, "row")
+    summed_rows = top_terms
+    for hop in (1, 2, 4):
+        summed_rows = summed_rows + lax.ppermute(
+            summed_rows, "row", [(dev, dev ^ hop) for dev in range(8)]
+        )
     top_share = lax.psum_scatter(summed_rows, "col", scatter_dimension=1, tiled=True)
     top_resid = (top_rhs.astype(jnp.float32) - top_share).astype(jnp.bfloat16)
     top_own = solve_piece(

time: 325 us -> 613 us (1.89)
  waiting for transfers between devices: 287 us -> 568 us
    ppermute x0 -> x3, waiting for transfers between devices: none -> 362 us  [local(): lax.ppermute(summed_rows, 'row', [(dev, dev ^ hop) for dev in range(8)])]
    psum x1 -> x0, waiting for transfers between devices: 81.3 us -> none  [local(): summed_rows = lax.psum(top_terms, 'row')]
  transfers between devices with their start and end apart: 5 -> 7, of which waited for: 5 -> 7; matrix products, arithmetic and copies ran while one was open for 0% -> 0% of each run, Pallas kernels for 0% -> 0%
where the time goes in v2:
time: 613 us
  waiting for transfers between devices  568 us (93%)
  between operations  14.7 us (2%)
  other arithmetic  12.1 us (2%)
  matrix products  9.55 us (2%)
    ppermute x3, waiting for transfers between devices, local(): lax.ppermute(summed_rows, 'row', [(dev, dev ^ hop) for dev in range(8)])  362 us
    reduce_scatter x1, waiting for transfers between devices, local(): lax.psum_scatter(mid_terms, 'row', scatter_dimension=1, tiled=True)  90.4 us
    all_gather x1, waiting for transfers between devices, local(): lax.all_gather(mid_resid, 'row', axis=1, tiled=True)  50.8 us
    reduce_scatter x1, waiting for transfers between devices, local(): lax.psum_scatter(summed_rows, 'col', scatter_dimension=1, tiled=True)  42.3 us
    all_gather x1, waiting for transfers between devices, local(): lax.all_gather(top_resid, 'col', axis=1, tiled=True)  22.1 us
  transfers between devices with their start and end apart: 7, of which 7 were waited for; matrix products, arithmetic and copies ran while one was open for 0% of the time, Pallas kernels for 0%

profile of v2, /device:TPU:0, one launch (start us, length us, event | category | flops | bytes accessed | tf_op | source)
XLA Modules:
  0.0 612.7 jit_solution(5992569962994428248)
XLA Ops:
  8.0 0.8 copy-done
  8.8 2.6 fusion.7
  11.4 1.0 copy-done.5
  12.4 1.3 fusion.4
  13.7 2.5 broadcast_select_fusion
  16.3 0.0 all-gather.3.cloned.1.call-start
  16.3 0.9 copy-done.3
  17.2 0.2 copy.12
  17.4 90.4 %reduce-scatter.3.cloned.1.call-done = f32[2,128,512]{1,2,0:T(8,128)} async-done(((f32[2,1024,512]{1,2,0:T(8,128)}), f32[2,128,512]{1,2,0:T(8,128)}) %reduce-scatter.3.cloned.1.call-update) | async-done | bytes 524304 | tf_op jit(solution)/shard_map/reduce_scatter | solution.py:32
  107.8 1.8 subtract_convert_fusion.1
  109.6 0.0 reduce-scatter.5.cloned.1.call-start
  109.7 50.8 %all-gather.3.cloned.1.call-done = bf16[2,1024,512]{1,2,0:T(8,128)(2,1)} async-done(((bf16[2,128,512]{1,2,0:T(8,128)(2,1)}), bf16[2,1024,512]{1,2,0:T(8,128)(2,1)}) %all-gather.3.cloned.1.call-update) | async-done | bytes 2097168 | tf_op jit(solution)/shard_map/all_gather | solution.py:35
  160.4 2.4 convolution_convert_fusion.1
  162.8 0.7 convolution_bitcast_fusion
  163.5 1.5 collective-permute-start
  165.0 90.7 %collective-permute-done = f32[2,1024,512]{1,2,0:T(8,128)S(1)} collective-permute-done((f32[2,1024,512]{1,2,0:T(8,128)S(1)}, f32[2,1024,512]{1,2,0:T(8,128)S(1)}, u32[]{:S(2)}, u32[]{:S(2)}) %collective-permute-start) | collective-permute-done | bytes 4194336 | tf_op jit(solution)/shard_map/ppermute | solution.py:42
  255.7 1.4 add.13
  257.1 0.1 collective-permute-start.1
  257.2 91.3 %collective-permute-done.1 = f32[2,1024,512]{1,2,0:T(8,128)S(1)} collective-permute-done((f32[2,1024,512]{1,2,0:T(8,128)S(1)}, f32[2,1024,512]{1,2,0:T(8,128)S(1)}, u32[]{:S(2)}, u32[]{:S(2)}) %collective-permute-start.1) | collective-permute-done | bytes 4194336 | tf_op jit(solution)/shard_map/ppermute | solution.py:42
  348.4 1.4 add.14
  349.8 0.8 collective-permute-start.2
  350.6 180.5 %collective-permute-done.2 = f32[2,1024,512]{1,2,0:T(8,128)S(1)} collective-permute-done((f32[2,1024,512]{1,2,0:T(8,128)S(1)}, f32[2,1024,512]{1,2,0:T(8,128)S(1)}, u32[]{:S(2)}, u32[]{:S(2)}) %collective-permute-start.2) | collective-permute-done | bytes 4194336 | tf_op jit(solution)/shard_map/ppermute | solution.py:42
  531.1 2.9 add.15
  534.0 0.0 all-gather.5.cloned.1.call-start
  534.0 1.0 copy-done.2
  535.0 0.2 copy.13
  535.2 42.3 %reduce-scatter.5.cloned.1.call-done = f32[2,256,512]{1,2,0:T(8,128)} async-done(((f32[2,1024,512]{1,2,0:T(8,128)}), f32[2,256,512]{1,2,0:T(8,128)}) %reduce-scatter.5.cloned.1.call-update) | async-done | bytes 1048592 | tf_op jit(solution)/shard_map/reduce_scatter | solution.py:45
  577.5 2.1 subtract_convert_fusion
  579.7 0.9 copy.14
  580.5 22.1 %all-gather.5.cloned.1.call-done = bf16[2,1024,512]{1,2,0:T(8,128)(2,1)} async-done(((bf16[2,256,512]{1,2,0:T(8,128)(2,1)}), bf16[2,1024,512]{1,2,0:T(8,128)(2,1)}) %all-gather.5.cloned.1.call-update) | async-done | bytes 2097168 | tf_op jit(solution)/shard_map/all_gather | solution.py:48
  602.6 2.6 fusion.10
  605.2 1.0 copy.15
  (14 shorter events, 0.1 us)
Async XLA Ops:
  7.2 1.6 copy-start
  7.2 100.6 %reduce-scatter.3.cloned.1.call-start = ((), (), s32[]{:S(2)}) async-start(), calls=%async_computation.2 | async-start | bytes 4718592 | tf_op jit(solution)/shard_map/reduce_scatter | solution.py:32
  8.8 3.6 copy-start.4
  11.4 1.0 copy-start.5
  16.2 0.9 copy-start.3
  16.3 144.2 %all-gather.3.cloned.1.call-start = ((), (), s32[]{:S(2)}) async-start(), calls=%async_computation.3 | async-start | bytes 2359296 | tf_op jit(solution)/shard_map/all_gather | solution.py:35
  17.4 145.5 %copy-start.1 = (bf16[2,1024,128]{2,1,0:T(8,128)(2,1)S(1)}, bf16[2,1024,128]{2,1,0:T(8,128)(2,1)}, u32[]{:S(2)}) copy-start(bf16[2,1024,128]{2,1,0:T(8,128)(2,1)} %param.14) | copy-start | bytes 1572868
  109.6 467.9 %reduce-scatter.5.cloned.1.call-start = ((), (), s32[]{:S(2)}) async-start(), calls=%async_computation.4 | async-start | bytes 5242880 | tf_op jit(solution)/shard_map/reduce_scatter | solution.py:45
  163.5 92.2 %collective-permute-start = (f32[2,1024,512]{1,2,0:T(8,128)S(1)}, f32[2,1024,512]{1,2,0:T(8,128)S(1)}, u32[]{:S(2)}, u32[]{:S(2)}) collective-permute-start(f32[2,1024,512]{1,2,0:T(8,128)S(1)} %convolution_bitcast_fusion), channel_id=1, source_target_pairs={{0,4},{4,0},{8,12},{12,8},{16,20},{20,16},{24,28},{28,24},{1,5},{5... | collective-permute-start | bytes 12582920 | tf_op jit(solution)/shard_map/ppermute | solution.py:42
  257.1 91.3 %collective-permute-start.1 = (f32[2,1024,512]{1,2,0:T(8,128)S(1)}, f32[2,1024,512]{1,2,0:T(8,128)S(1)}, u32[]{:S(2)}, u32[]{:S(2)}) collective-permute-start(f32[2,1024,512]{1,2,0:T(8,128)S(1)} %add.13), channel_id=1, source_target_pairs={{0,8},{4,12},{8,0},{12,4},{16,24},{20,28},{24,16},{28,20},{1,9},{5... | collective-permute-start | bytes 12582920 | tf_op jit(solution)/shard_map/ppermute | solution.py:42
  349.8 181.3 %collective-permute-start.2 = (f32[2,1024,512]{1,2,0:T(8,128)S(1)}, f32[2,1024,512]{1,2,0:T(8,128)S(1)}, u32[]{:S(2)}, u32[]{:S(2)}) collective-permute-start(f32[2,1024,512]{1,2,0:T(8,128)S(1)} %add.14), channel_id=1, source_target_pairs={{0,16},{4,20},{8,24},{12,28},{16,0},{20,4},{24,8},{28,12},{1,17},{... | collective-permute-start | bytes 12582920 | tf_op jit(solution)/shard_map/ppermute | solution.py:42
  534.0 1.0 copy-start.2
  534.0 68.7 %all-gather.5.cloned.1.call-start = ((), (), s32[]{:S(2)}) async-start(), calls=%async_computation.5 | async-start | bytes 2621440 | tf_op jit(solution)/shard_map/all_gather | solution.py:48
Sparse Core Ops, SparseCore 0:
  16.4 91.3 reduce-scatter.2
  110.4 49.9 all-gather.2
  534.1 43.3 reduce-scatter.4
  579.8 22.8 all-gather.4
